TPU v7x, 32 devices: a whole 2x2x4 slice. The times are simulated.
32 devices in a mesh: pb: 8 (over z, x), row: 4 (over y, core).
Axes of the slice: x: 2, y: 2, z: 4, core: 2. Of those that a mesh axis runs over, the one named last changes fastest.
Arguments:
- kernels: bfloat16 [8, 4096, 4096], P('pb', 'row'), may hold values from -6 to 6
- orbitals: bfloat16 [4096, 1024], P('pb'), may hold values from -0.75 to 0.75
- pairs: int32 [8, 4, 2], replicated, may hold values from 0 to 15
- k_slot: int32 [16], replicated, may hold values from 0 to 15, each once
- pair_count: int32 [8], replicated, may hold values from 1 to 4, as said below
Outputs:
- exchange_fields: float32 [4, 1024, 1024], P('row', 'pb')
Inputs may be any that keep to these rules, and one draw needn't show every extreme that they name: `k_slot`: every slot holds exactly one k-point. pairs p < pair_count[q] are live; some transfer vector has all 4 live.
All inputs are finite; a program needn't handle non-finite values.
Results may differ from a plain program's by a relative error of at most 0.0029.
Values may be sent and summed in bfloat16 or wider, within the bound.
A program may use at most 128 MiB of HBM per device.

v0:
```python
import jax
import jax.numpy as jnp
from jax import lax
from jax.sharding import PartitionSpec as P


def slot_lookup(k_ids, k_slot):
    positions = jnp.arange(k_slot.shape[0], dtype=jnp.int32)
    return jnp.sum(jnp.where(k_ids[..., None] == positions, k_slot, 0), axis=-1)


def pair_products(weight, orbital_basis, pair_index, orb_width, pair_total, row_start, row_count):
    orb_left = lax.dynamic_slice_in_dim(orbital_basis, pair_index * orb_width, orb_width, 1)
    orb_right = lax.dynamic_slice_in_dim(
        orbital_basis, (pair_total + pair_index) * orb_width, orb_width, 1
    )
    left_rows = lax.dynamic_slice_in_dim(orb_left, row_start, row_count, 0)
    right_rows = lax.dynamic_slice_in_dim(orb_right, row_start, row_count, 0)
    contract = (((1,), (1,)), ((), ()))
    right_gram = lax.dot_general(
        right_rows, orb_right, contract, preferred_element_type=jnp.float32
    )
    first_term = jnp.dot(
        (weight * right_gram).astype(jnp.bfloat16), orb_left, preferred_element_type=jnp.float32
    )
    left_gram = lax.dot_general(left_rows, orb_left, contract, preferred_element_type=jnp.float32)
    second_hadamard = (weight * left_gram).astype(jnp.bfloat16)
    second_term = lax.dot_general(
        second_hadamard, right_rows, (((0,), (0,)), ((), ())), preferred_element_type=jnp.float32
    )
    return (first_term, second_term)


def shards(kernels, orbitals, pairs, k_slot, pair_count):
    pb_count = lax.axis_size("pb")
    row_devices = lax.axis_size("row")
    here_row = lax.axis_index("row")
    weight = kernels[0]
    row_count = weight.shape[0]
    point_total = weight.shape[1]
    pair_total = pairs.shape[1]
    k_total = k_slot.shape[0]
    orb_width = orbitals.shape[1] // k_total
    local_points = orbitals.shape[0]
    local_orbs = orbitals.reshape(local_points, k_total, orb_width)
    wanted = jnp.concatenate(
        [slot_lookup(pairs[:, :, 0], k_slot), slot_lookup(pairs[:, :, 1], k_slot)], axis=1
    )
    slot_share = 2 * pair_total // row_devices
    my_slots = lax.dynamic_slice_in_dim(wanted, here_row * slot_share, slot_share, 1)
    picked = jnp.take(local_orbs, my_slots, axis=1).reshape(
        local_points, pb_count, slot_share * orb_width
    )
    arrived_orbs = lax.all_to_all(picked, "pb", split_axis=1, concat_axis=0, tiled=True)
    orbital_basis = lax.all_gather(
        arrived_orbs.reshape(point_total, slot_share * orb_width), "row", axis=1, tiled=True
    )
    row_start = here_row * row_count
    first_list = []
    second_list = []
    for pair_index in range(pair_total):
        first_term, second_term = pair_products(
            weight, orbital_basis, pair_index, orb_width, pair_total, row_start, row_count
        )
        first_list.append(first_term)
        second_list.append(second_term)
    first_block = jnp.concatenate(first_list, axis=1)
    second_block = jnp.concatenate(second_list, axis=1)
    second_whole = lax.psum(second_block, "row")
    second_rows = lax.dynamic_slice_in_dim(second_whole, row_start, row_count, 0)
    contrib = jnp.concatenate([first_block, second_rows], axis=1)
    arrived = lax.all_to_all(contrib, "pb", split_axis=0, concat_axis=1, tiled=True)
    point_share = row_count // pb_count
    arrived = arrived.reshape(point_share, pb_count * 2 * pair_total, orb_width)
    targets = jnp.concatenate([pairs[:, :, 0], pairs[:, :, 1]], axis=1)
    pair_ids = jnp.arange(pair_total, dtype=jnp.int32)
    live_half = pair_ids[None, :] < pair_count[:, None]
    live_mask = jnp.concatenate([live_half, live_half], axis=1)
    k_ids = jnp.arange(k_total, dtype=jnp.int32)
    onehot = jnp.where((targets[..., None] == k_ids) & live_mask[..., None], 1.0, 0.0).astype(
        jnp.float32
    )
    onehot = onehot.reshape(pb_count * 2 * pair_total, k_total)
    fields = jnp.einsum("msn,sk->mkn", arrived, onehot, precision=lax.Precision.HIGHEST)
    return fields.reshape(1, point_share, k_total * orb_width)


def solution(mesh):
    placed = (P("pb", "row", None), P("pb", None), P(), P(), P())
    return jax.shard_map(
        shards, mesh=mesh, in_specs=placed, out_specs=P("row", "pb", None), check_vma=False
    )
```

profile of v0, /device:TPU:0, one launch (start us, length us, event | category | flops | bytes accessed | tf_op | source)
XLA Modules:
  0.0 276.9 jit_solution(14889424699236633594)
XLA Ops:
  6.5 0.8 fusion.76
  7.3 0.9 select_reduce_fusion.1
  8.7 1.5 copy.20
  10.2 0.6 gather_fusion
  11.1 32.8 %all_to_all.31 = bf16[512,8,128]{0,2,1:T(8,128)(2,1)S(1)} all-to-all(bf16[512,8,128]{0,2,1:T(8,128)(2,1)S(1)} %broadcast_select_fusion), channel_id=1, replica_groups=mesh['pb'=8,'row'=4] {'pb'}, dimensions={1} | all-to-all | bytes 2097152 | tf_op jit(solution)/shard_map/all_to_all | solution.py:54
  43.9 1.3 copy.22
  45.3 34.1 %all-gather.2.cloned.1.call-done = bf16[4096,512]{1,0:T(8,128)(2,1)} async-done(((bf16[4096,128]{1,0:T(8,128)(2,1)}), bf16[4096,512]{1,0:T(8,128)(2,1)}) %all-gather.2.cloned.1.call-update) | async-done | bytes 4194320 | tf_op jit(solution)/shard_map/all_gather | solution.py:55
  79.4 5.8 %fusion.75 = (bf16[4096,64]{1,0:T(8,128)(2,1)}, bf16[4096,64]{1,0:T(8,128)(2,1)}, bf16[4096,64]{1,0:T(8,128)(2,1)S(1)}, bf16[4096,64]{1,0:T(8,128)(2,1)}, bf16[4...) fusion(bf16[4096,512]{1,0:T(8,128)(2,1)} %all-gather.2.cloned.1.c, ...), kind=kLoop, calls=%fused_computation.82 | loop fusion | bytes 8388608 | tf_op jit(solution)/shard_map/dynamic_slice | solution.py:13
  85.3 9.3 %fusion.11 = f32[4096,64]{0,1:T(8,128)} fusion(bf16[4096,64]{1,0:T(8,128)(2,1)} %get-tuple-element.9, bf16[1,1024,4096]{2,1,0:T(8,128)(2,1)} %param.5, s32[]{:T(128)S(6)} %select_n.42, bf16[4096,64]{1,0:T(8,128)(2,1)} %get-tuple-element.16), kind=kOutput, calls=%fused_computation.21 | convolution fusion | flops 1086324736 | bytes 11011072 | tf_op jit(solution)/shard_map/dot_general | solution.py:28
  94.5 8.6 %fusion.8 = f32[4096,64]{0,1:T(8,128)} fusion(bf16[4096,64]{1,0:T(8,128)(2,1)} %get-tuple-element.10, bf16[1,1024,4096]{2,1,0:T(8,128)(2,1)} %param.5, s32[]{:T(128)S(6)} %select_n.42, bf16[4096,64]{1,0:T(8,128)(2,1)S(1)} %get-tuple-element.11), kind=kOutput, calls=%fused_computation.18 | convolution fusion | flops 1086324736 | bytes 11011072 | tf_op jit(solution)/shard_map/dot_general | solution.py:28
  103.1 8.5 %fusion.9 = f32[4096,64]{0,1:T(8,128)} fusion(bf16[4096,64]{1,0:T(8,128)(2,1)} %get-tuple-element.12, bf16[1,1024,4096]{2,1,0:T(8,128)(2,1)} %param.5, s32[]{:T(128)S(6)} %select_n.42, bf16[4096,64]{1,0:T(8,128)(2,1)S(1)} %get-tuple-element.13), kind=kOutput, calls=%fused_computation.19 | convolution fusion | flops 1086324736 | bytes 11011072 | tf_op jit(solution)/shard_map/dot_general | solution.py:28
  111.7 8.8 %fusion.10 = f32[4096,64]{0,1:T(8,128)} fusion(bf16[4096,64]{1,0:T(8,128)(2,1)} %get-tuple-element.14, bf16[1,1024,4096]{2,1,0:T(8,128)(2,1)} %param.5, s32[]{:T(128)S(6)} %select_n.42, bf16[4096,64]{1,0:T(8,128)(2,1)S(1)} %get-tuple-element.15), kind=kOutput, calls=%fused_computation.20 | convolution fusion | flops 1086324736 | bytes 11011072 | tf_op jit(solution)/shard_map/dot_general | solution.py:28
  120.5 4.3 %pad_maximum_fusion = f32[4096,256]{0,1:T(8,128)} fusion(f32[4096,64]{0,1:T(8,128)} %fusion.8, f32[4096,64]{0,1:T(8,128)} %fusion.9, f32[4096,64]{0,1:T(8,128)} %fusion.10, f32[4096,64]{0,1:T(8,128)S(1)} %copy-done.2), kind=kLoop, calls=%fused_computation.17 | loop fusion | flops 3145728 | bytes 8388608 | tf_op jit(solution)/shard_map/concatenate | solution.py:68
  124.8 8.8 %fusion.21 = f32[1024,512]{0,1:T(8,128)S(1)} fusion(bf16[4096,64]{1,0:T(8,128)(2,1)} %get-tuple-element.16, bf16[1,1024,4096]{2,1,0:T(8,128)(2,1)} %param.5, s32[]{:T(128)S(6)} %select_n.42, bf16[4096,512]{1,0:T(8,128)(2,1)} %all-gather.2.cloned.1.call-done), kind=kOutput, calls=%fused_computation.30 | convolution fusion | flops 1086324736 | bytes 11010052 | tf_op jit(solution)/shard_map/dot_general | solution.py:23
  133.6 8.9 %fusion.22 = f32[1024,512]{0,1:T(8,128)S(1)} fusion(f32[1024,512]{0,1:T(8,128)S(1)} %fusion.21, bf16[4096,64]{1,0:T(8,128)(2,1)} %copy-done.1, bf16[1,1024,4096]{2,1,0:T(8,128)(2,1)} %param.5, s32[]{:T(128)S(6)} %select_n.42, bf16[4096,512]{1,0:T(8,128)(2,1)} %all-gather.2.cloned.1.call-done), kind=kOutput, calls=%fused_computation.31 | convolution fusion | flops 1086324736 | bytes 11010052 | tf_op jit(solution)/shard_map/dot_general | solution.py:23
  142.5 9.2 %fusion.23 = f32[1024,512]{0,1:T(8,128)S(1)} fusion(f32[1024,512]{0,1:T(8,128)S(1)} %fusion.22, bf16[4096,64]{1,0:T(8,128)(2,1)} %copy-done, bf16[1,1024,4096]{2,1,0:T(8,128)(2,1)} %param.5, s32[]{:T(128)S(6)} %select_n.42, bf16[4096,512]{1,0:T(8,128)(2,1)} %all-gather.2.cloned.1.call-done), kind=kOutput, calls=%fused_computation.32 | convolution fusion | flops 1086324736 | bytes 11010052 | tf_op jit(solution)/shard_map/dot_general | solution.py:23
  151.7 8.5 %fusion.24 = f32[1024,512]{0,1:T(8,128)S(1)} fusion(f32[1024,512]{0,1:T(8,128)S(1)} %fusion.23, bf16[4096,64]{1,0:T(8,128)(2,1)S(1)} %get-tuple-element.11, bf16[1,1024,4096]{2,1,0:T(8,128)(2,1)} %param.5, s32[]{:T(128)S(6)} %select_n.42, bf16[4096,512]{1,0:T(8,128)(2,1)} %all-gather.2.cloned.1.call-done), kind=kOutput, calls=%fused_computation.33 | convolution fusion | flops 1086324736 | bytes 11010052 | tf_op jit(solution)/shard_map/dot_general | solution.py:23
  160.2 50.3 %all-reduce.2.cloned.1.call-done = f32[4096,256]{0,1:T(8,128)} async-done(((f32[4096,256]{0,1:T(8,128)}), f32[4096,256]{0,1:T(8,128)}) %all-reduce.2.cloned.1.call-update) | async-done | bytes 4194320 | tf_op jit(solution)/shard_map/psum | solution.py:69
  210.5 1.3 dynamic-slice_dynamic-update-slice_fusion
  211.8 1.5 copy_bitcast_fusion
  213.3 5.5 %all-to-all-start.1 = ((f32[8,128,512]{1,2,0:T(8,128)}), f32[8,128,512]{1,2,0:T(8,128)S(1)}, u32[]{:S(2)}, u32[]{:S(2)}) async-start(f32[8,128,512]{1,2,0:T(8,128)} %copy_bitcast_fusion), calls=%async_computation.1 | async-start | bytes 4194304 | tf_op jit(solution)/shard_map/all_to_all | solution.py:72
  219.2 47.5 %all-to-all-done.1 = f32[8,128,512]{1,2,0:T(8,128)S(1)} async-done(((f32[8,128,512]{1,2,0:T(8,128)}), f32[8,128,512]{1,2,0:T(8,128)S(1)}, u32[]{:S(2)}, u32[]{:S(2)}) %all-to-all-start.1) | async-done | bytes 2097184 | tf_op jit(solution)/shard_map/all_to_all | solution.py:72
  266.7 2.2 fusion.18
  269.1 1.0 copy.26
  (28 shorter events, 1.3 us)
Async XLA Ops:
  6.5 72.9 %all-gather.2.cloned.1.call-start = ((), (), s32[]{:S(2)}) async-start(), calls=%async_computation.2 | async-start | bytes 5242880 | tf_op jit(solution)/shard_map/all_gather | solution.py:55
  45.2 165.2 %all-reduce.2.cloned.1.call-start = ((), (), s32[]{:S(2)}) async-start(), calls=%async_computation.3 | async-start | bytes 8388608 | tf_op jit(solution)/shard_map/psum | solution.py:69
  85.2 17.9 %copy-start = (bf16[4096,64]{1,0:T(8,128)(2,1)}, bf16[4096,64]{1,0:T(8,128)(2,1)S(1)}, u32[]{:S(2)}) copy-start(bf16[4096,64]{1,0:T(8,128)(2,1)S(1)} %get-tuple-element.13) | copy-start | bytes 1572868
  85.2 26.4 %copy-start.1 = (bf16[4096,64]{1,0:T(8,128)(2,1)}, bf16[4096,64]{1,0:T(8,128)(2,1)S(1)}, u32[]{:S(2)}) copy-start(bf16[4096,64]{1,0:T(8,128)(2,1)S(1)} %get-tuple-element.15) | copy-start | bytes 1572868
  111.7 8.8 %copy-start.2 = (f32[4096,64]{0,1:T(8,128)S(1)}, f32[4096,64]{0,1:T(8,128)}, u32[]{:S(2)}) copy-start(f32[4096,64]{0,1:T(8,128)} %fusion.11) | copy-start | bytes 3145732
  151.7 67.1 %copy-start.3 = (s32[8]{0:T(128)S(1)}, s32[8]{0:T(128)}, u32[]{:S(2)}) copy-start(s32[8]{0:T(128)} %param.9) | copy-start | bytes 100
  213.3 53.4 %all-to-all-start.1 = ((f32[8,128,512]{1,2,0:T(8,128)}), f32[8,128,512]{1,2,0:T(8,128)S(1)}, u32[]{:S(2)}, u32[]{:S(2)}) async-start(f32[8,128,512]{1,2,0:T(8,128)} %copy_bitcast_fusion), calls=%async_computation.1 | async-start | bytes 4194304 | tf_op jit(solution)/shard_map/all_to_all | solution.py:72
Sparse Core Ops, SparseCore 0:
  45.3 34.0 all-gather.1
  124.9 85.4 all-reduce.1
where the time goes:
time: 277 us
  waiting for transfers between devices  132 us (48%)
  matrix products  72.9 us (26%)
  blocking collectives  32.8 us (12%)
  local copies, waits for them, and re-layouts  14.6 us (5%)
  between operations  13.5 us (5%)
  other arithmetic  5.63 us (2%)
  starting transfers between devices  5.55 us (2%)
    psum x1, waiting for transfers between devices, shards(): second_whole = lax.psum(second_block, 'row')  50.3 us
    all_to_all x1, waiting for transfers between devices, shards(): lax.all_to_all(contrib, 'pb', split_axis=0, concat_axis=1, tiled=True)  47.5 us
    dot_general x4, matrix products, pair_products(): jnp.dot((weight * right_gram).astype(jnp.bfloat16), orb_left, preferred_e...  35.4 us
    dot_general x4, matrix products, pair_products(): lax.dot_general(second_hadamard, right_rows, (((0,), (0,)), ((), ())), pr...  35.2 us
    all_gather x1, waiting for transfers between devices, shards(): lax.all_gather(arrived_orbs.reshape(point_total, slot_share * orb_width),...  34.1 us
    all_to_all x1, blocking collectives, shards(): lax.all_to_all(picked, 'pb', split_axis=1, concat_axis=0, tiled=True)  32.8 us
    dynamic_slice x1, local copies, waits for them, and re-layouts, pair_products(): lax.dynamic_slice_in_dim(orbital_basis, pair_index * orb_width, orb_width...  5.82 us
  transfers between devices with their start and end apart: 3, of which 3 were waited for; matrix products, arithmetic and copies ran while one was open for 13% of the time, Pallas kernels for 0%

commit v1 on v0

v1 whole, which is shorter than its diff:
```python
import functools

import jax
import jax.numpy as jnp
from jax import lax
from jax.experimental import pallas as pl
from jax.experimental.pallas import tpu as pltpu
from jax.sharding import PartitionSpec as P

MESH = pl.DeviceIdType.MESH
BF16 = jnp.bfloat16
F32 = jnp.float32
NT = (((1,), (1,)), ((), ()))


def pick_kernel(width, pairs_ref, slot_ref, orb_ref, out_ref):
    pair_total, pb_count, half, lanes = out_ref.shape
    part = lax.rem(lax.axis_index("row"), 2)
    rows = pl.ds(pl.multiple_of(part * half, half), half)
    low = lax.broadcasted_iota(jnp.int32, (half, lanes), 1) < width

    def fetch(k, want):
        slot = slot_ref[k]
        block = orb_ref[rows, pl.ds(pl.multiple_of((slot >> 1) * lanes, lanes), lanes)].astype(F32)
        moved = pltpu.roll(block, width, 1)
        return jnp.where((slot & 1) == want, block, moved)

    def step(n, carry):
        q, p = lax.rem(n, pb_count), lax.div(n, pb_count)
        left = fetch(pairs_ref[q, p, 0], 0)
        right = fetch(pairs_ref[q, p, 1], 1)
        out_ref[p, q] = jnp.where(low, left, right).astype(BF16)
        return carry

    lax.fori_loop(0, pair_total * pb_count, step, 0)


def main_kernel(dims, picked, kern, out, w, basis, rows_r, rows_l, rows_t, f1, f2s, f2r, cbuf,
                w_sem, d_send, d_recv, g_send, g_recv, s_send, s_recv, c_send, c_recv):
    pb_count, row_devices, pair_total, half, tile, width = dims
    pb, row = lax.axis_index("pb"), lax.axis_index("row")
    part = lax.rem(row, 2)
    mate = row + 1 - 2 * part
    row_count, point_total = w.shape
    lanes = basis.shape[2]
    share = row_count // pb_count
    tiles = point_total // tile
    per_chunk = row_count // tile

    w_copy = pltpu.make_async_copy(kern.at[0], w, w_sem)
    w_copy.start()

    barrier = pltpu.get_barrier_semaphore()

    def greet_pb(d, c):
        pl.semaphore_signal(barrier, inc=1, device_id=(lax.rem(pb + d, pb_count), row), device_id_type=MESH)
        return c

    def greet_row(d, c):
        pl.semaphore_signal(barrier, inc=1, device_id=(pb, lax.rem(row + d, row_devices)), device_id_type=MESH)
        return c

    lax.fori_loop(1, pb_count, greet_pb, 0)
    lax.fori_loop(1, row_devices, greet_row, 0)
    pl.semaphore_wait(barrier, pb_count + row_devices - 2)

    def block_rows(j, which):
        return pl.ds(pl.multiple_of((j * 2 + which) * half, half), half)

    def own(p):
        return pltpu.make_async_copy(picked.at[p, pb], basis.at[p, block_rows(pb, part)], d_recv.at[p, 0])

    def direct(p, d):
        q = lax.rem(pb + d, pb_count)
        return pltpu.make_async_remote_copy(
            src_ref=picked.at[p, q], dst_ref=basis.at[p, block_rows(pb, part)],
            send_sem=d_send.at[p, d], recv_sem=d_recv.at[p, d],
            device_id=(q, row), device_id_type=MESH)

    def relay(p, d):
        j = lax.rem(pb + pb_count - d, pb_count)
        spot = basis.at[p, block_rows(j, part)]
        return pltpu.make_async_remote_copy(
            src_ref=spot, dst_ref=spot, send_sem=g_send.at[p, d], recv_sem=g_recv.at[p, d],
            device_id=(pb, mate), device_id_type=MESH)

    def shed(p, d):
        to = lax.rem(row + d, row_devices)
        return pltpu.make_async_remote_copy(
            src_ref=f2s.at[p, to], dst_ref=f2r.at[p, d], send_sem=s_send.at[p, d], recv_sem=s_recv.at[p, d],
            device_id=(pb, to), device_id_type=MESH)

    def c_rows(j):
        return pl.ds(pl.multiple_of(j * share, share), share)

    def own_c(p):
        return pltpu.make_async_copy(cbuf.at[p, c_rows(pb)], out.at[p, pb], c_recv.at[p, 0])

    def give(p, d):
        j = lax.rem(pb + d, pb_count)
        return pltpu.make_async_remote_copy(
            src_ref=cbuf.at[p, c_rows(j)], dst_ref=out.at[p, pb], send_sem=c_send.at[p, d], recv_sem=c_recv.at[p, d],
            device_id=(j, row), device_id_type=MESH)

    def loop(low, high, body):
        def step(i, c):
            body(i)
            return c
        lax.fori_loop(low, high, step, 0)

    def send_pair(p):
        own(p).start()
        loop(1, pb_count, lambda d: direct(p, d).start())

    loop(0, pair_total, send_pair)

    def relay_pair(p):
        own(p).wait()
        relay(p, 0).start()

        def one(d):
            direct(p, d).wait_recv()
            relay(p, d).start()

        loop(1, pb_count, one)

    low = lax.broadcasted_iota(jnp.int32, (row_count, lanes), 1) < width

    def finish_pair(p):
        total = f2s[p, row].astype(F32)
        for d in range(1, row_devices):
            shed(p, d).wait_recv()
            total = total + f2r[p, d].astype(F32)
        stacked = jnp.concatenate([jnp.zeros_like(total), total], axis=0)
        cbuf[p] = jnp.where(low, f1[p], stacked.T).astype(BF16)
        own_c(p).start()
        loop(1, pb_count, lambda d: give(p, d).start())

    def tiles_of(p, start, stop):
        def one(t):
            cols = pl.ds(pl.multiple_of(t * tile, tile), tile)
            there = basis[p, cols, :]
            second = None
            chunk = row_count // 2
            for m in range(2):
                here = slice(m * chunk, (m + 1) * chunk)
                weight = w[here, cols].astype(F32)
                gram = lax.dot_general(rows_r[here], there, NT, preferred_element_type=F32)
                f1[p, here] += jnp.dot((weight * gram).astype(BF16), there, preferred_element_type=F32)
                gram = lax.dot_general(rows_l[here], there, NT, preferred_element_type=F32)
                term = jnp.dot(rows_t[:, here], (weight * gram).astype(BF16), preferred_element_type=F32)
                second = term if second is None else second + term
            inner = pl.ds(pl.multiple_of(lax.rem(t, per_chunk) * tile, tile), tile)
            f2s[p, lax.div(t, per_chunk), :, inner] = second[width:].astype(BF16)

        loop(start, stop, one)

    relay_pair(0)
    w_copy.wait()

    def pair_step(p):
        loop(0, pb_count, lambda d: relay(p, d).wait_recv())
        mine = basis[p, pl.ds(pl.multiple_of(row * row_count, row_count), row_count), :]
        rows_r[...] = jnp.where(low, 0, mine.astype(F32)).astype(BF16)
        rows_l[...] = jnp.where(low, mine.astype(F32), 0).astype(BF16)
        rows_t[...] = mine.astype(F32).T.astype(BF16)
        f1[p] = jnp.zeros((row_count, lanes), F32)
        tiles_of(p, 0, tiles // 2)

        @pl.when(p + 1 < pair_total)
        def _():
            relay_pair(p + 1)

        @pl.when(p > 0)
        def _():
            finish_pair(p - 1)

        tiles_of(p, tiles // 2, tiles)
        loop(1, row_devices, lambda d: shed(p, d).start())

    loop(0, pair_total, pair_step)
    finish_pair(pair_total - 1)

    def settle(p):
        own_c(p).wait()
        relay(p, 0).wait_send()

        def one(d):
            direct(p, d).wait_send()
            relay(p, d).wait_send()
            give(p, d).wait()

        loop(1, pb_count, one)
        loop(1, row_devices, lambda d: shed(p, d).wait_send())

    loop(0, pair_total, settle)


def combine_kernel(width, pairs_ref, count_ref, got_ref, out_ref):
    pair_total, pb_count, share, lanes = got_ref.shape
    low = lax.broadcasted_iota(jnp.int32, (share, lanes), 1) < width
    out_ref[...] = jnp.zeros_like(out_ref)

    def step(n, carry):
        q, p = lax.rem(n, pb_count), lax.div(n, pb_count)

        @pl.when(p < count_ref[q])
        def _():
            block = got_ref[p, q].astype(F32)
            moved = pltpu.roll(block, width, 1)
            for side in range(2):
                k = pairs_ref[q, p, side]
                odd = k & 1
                value = jnp.where(odd == side, block, moved)
                value = jnp.where(low == (odd == 0), value, 0.0)
                spot = pl.ds(pl.multiple_of((k >> 1) * lanes, lanes), lanes)
                out_ref[0, :, spot] += value

        return carry

    lax.fori_loop(0, pair_total * pb_count, step, 0)


def shards(kernels, orbitals, pairs, k_slot, pair_count):
    pb_count, row_devices = lax.axis_size("pb"), lax.axis_size("row")
    row_count, point_total = kernels.shape[1:]
    pair_total = pairs.shape[1]
    k_total = k_slot.shape[0]
    width = orbitals.shape[1] // k_total
    lanes = 2 * width
    half = orbitals.shape[0] // 2
    share = row_count // pb_count
    tile = row_count // 2
    smem = pl.BlockSpec(memory_space=pltpu.SMEM)
    vmem = pl.BlockSpec(memory_space=pltpu.VMEM)
    hbm = pl.BlockSpec(memory_space=pl.ANY)
    picked = pl.pallas_call(
        functools.partial(pick_kernel, width),
        out_shape=jax.ShapeDtypeStruct((pair_total, pb_count, half, lanes), BF16),
        in_specs=[smem, smem, vmem],
        out_specs=vmem,
    )(pairs, k_slot, orbitals)
    sems = pltpu.SemaphoreType.DMA
    got = pl.pallas_call(
        functools.partial(main_kernel, (pb_count, row_devices, pair_total, half, tile, width)),
        out_shape=jax.ShapeDtypeStruct((pair_total, pb_count, share, lanes), BF16),
        in_specs=[hbm, hbm],
        out_specs=hbm,
        scratch_shapes=[
            pltpu.VMEM((row_count, point_total), BF16),
            pltpu.VMEM((pair_total, point_total, lanes), BF16),
            pltpu.VMEM((row_count, lanes), BF16),
            pltpu.VMEM((row_count, lanes), BF16),
            pltpu.VMEM((lanes, row_count), BF16),
            pltpu.VMEM((pair_total, row_count, lanes), F32),
            pltpu.VMEM((pair_total, row_devices, width, row_count), BF16),
            pltpu.VMEM((pair_total, row_devices, width, row_count), BF16),
            pltpu.VMEM((pair_total, row_count, lanes), BF16),
            sems,
            sems((pair_total, pb_count)),
            sems((pair_total, pb_count)),
            sems((pair_total, pb_count)),
            sems((pair_total, pb_count)),
            sems((pair_total, row_devices)),
            sems((pair_total, row_devices)),
            sems((pair_total, pb_count)),
            sems((pair_total, pb_count)),
        ],
        compiler_params=pltpu.CompilerParams(
            collective_id=0, has_side_effects=True, vmem_limit_bytes=56 * 1024 * 1024
        ),
    )(picked, kernels)
    return pl.pallas_call(
        functools.partial(combine_kernel, width),
        out_shape=jax.ShapeDtypeStruct((1, share, k_total * width), F32),
        in_specs=[smem, smem, vmem],
        out_specs=vmem,
    )(pairs, pair_count, got)


def solution(mesh):
    placed = (P("pb", "row", None), P("pb", None), P(), P(), P())
    return jax.shard_map(
        shards, mesh=mesh, in_specs=placed, out_specs=P("row", "pb", None), check_vma=False
    )
```

time: 277 us -> 107 us (0.39)
  waiting for transfers between devices: 132 us -> 0 us
  Pallas kernels: 0 us -> 105 us
  matrix products: 72.9 us -> 0 us
  blocking collectives: 32.8 us -> 0 us
  between operations: 13.5 us -> 0.01 us
  local copies, waits for them, and re-layouts: 14.6 us -> 1.37 us
  other arithmetic: 5.63 us -> 0 us
  starting transfers between devices: 5.55 us -> 0 us
    pallas_call x0 -> x3, Pallas kernels: none -> 105 us  [the longest x1 94.1 us: shards(): pl.pallas_call(functools.partial(main_kernel, (pb_count, row_devices, pai...]
    dot_general x9 -> x0, matrix products: 72.9 us -> none  [the longest x4 35.4 us: pair_products(): jnp.dot((weight * right_gram).astype(jnp.bfloat16), orb_left, preferred_e...]
    psum x1 -> x0, waiting for transfers between devices: 50.3 us -> none  [shards(): second_whole = lax.psum(second_block, 'row')]
    all_to_all x1 -> x0, waiting for transfers between devices: 47.5 us -> none  [shards(): lax.all_to_all(contrib, 'pb', split_axis=0, concat_axis=1, tiled=True)]
    all_gather x1 -> x0, waiting for transfers between devices: 34.1 us -> none  [shards(): lax.all_gather(arrived_orbs.reshape(point_total, slot_share * orb_width),...]
    all_to_all x1 -> x0, blocking collectives: 32.8 us -> none  [shards(): lax.all_to_all(picked, 'pb', split_axis=1, concat_axis=0, tiled=True)]
    dynamic_slice x1 -> x0, local copies, waits for them, and re-layouts: 5.82 us -> none  [pair_products(): lax.dynamic_slice_in_dim(orbital_basis, pair_index * orb_width, orb_width...]
    all_to_all x1 -> x0, starting transfers between devices: 5.51 us -> none  [shards(): lax.all_to_all(contrib, 'pb', split_axis=0, concat_axis=1, tiled=True)]
  transfers between devices with their start and end apart: 3 -> 0, of which waited for: 3 -> 0; matrix products, arithmetic and copies ran while one was open for 13% -> 0% of each run, Pallas kernels for 0% -> 0%
where the time goes in v1:
time: 107 us
  Pallas kernels  105 us (98%)
  local copies, waits for them, and re-layouts  1.37 us (1%)
    pallas_call x1, Pallas kernels, shards(): pl.pallas_call(functools.partial(main_kernel, (pb_count, row_devices, pai...  94.1 us
    pallas_call x1, Pallas kernels, shards(): pl.pallas_call(functools.partial(pick_kernel, width), out_shape=jax.Shape...  6.49 us
    pallas_call x1, Pallas kernels, shards(): pl.pallas_call(functools.partial(combine_kernel, width), out_shape=jax.Sh...  4.71 us

profile of v1, /device:TPU:0, one launch (start us, length us, event | category | flops | bytes accessed | tf_op | source)
XLA Modules:
  0.0 106.7 jit_solution(11600991864822166706)
XLA Ops:
  0.0 1.4 %copy.7.pairs_ref = s32[8,4,2]{2,1,0:T(4,128)} copy(s32[8,4,2]{0,2,1:T(2,128)} %param.7) | data formatting | bytes 512 | tf_op args[2]
  1.4 6.5 %shard_map.55.picked = bf16[4,8,256,128]{3,2,1,0:T(8,128)(2,1)} custom-call(s32[8,4,2]{2,1,0:T(4,128)} %copy.7.pairs_ref, s32[16]{0:T(128)} %slot_ref.1, bf16[512,1024]{1,0:T(8,128)(2,1)} %orb_ref.1), custom_call_target="tpu_custom_call" | custom-call | tf_op jit(solution)/shard_map/pallas_call | solution.py:237
  7.9 94.1 %shard_map.56.got_ref = bf16[4,8,128,128]{3,2,1,0:T(8,128)(2,1)} custom-call(bf16[4,8,256,128]{3,2,1,0:T(8,128)(2,1)} %shard_map.55.picked, bf16[1,1024,4096]{2,1,0:T(8,128)(2,1)} %kern.1), custom_call_target="tpu_custom_call" | custom-call | tf_op jit(solution)/shard_map/pallas_call | solution.py:244
  101.9 4.7 %shard_map.57 = f32[1,128,1024]{2,1,0:T(8,128)} custom-call(s32[8,4,2]{2,1,0:T(4,128)} %copy.7.pairs_ref, s32[8]{0:T(128)} %count_ref.1, bf16[4,8,128,128]{3,2,1,0:T(8,128)(2,1)} %shard_map.56.got_ref), custom_call_target="tpu_custom_call" | custom-call | tf_op jit(solution)/shard_map/pallas_call | solution.py:273

commit v2 on v1

--- a/solution.py
+++ b/solution.py
@@ -14,10 +14,9 @@
 
 
 def pick_kernel(width, pairs_ref, slot_ref, orb_ref, out_ref):
-    pair_total, pb_count, half, lanes = out_ref.shape
-    part = lax.rem(lax.axis_index("row"), 2)
-    rows = pl.ds(pl.multiple_of(part * half, half), half)
-    low = lax.broadcasted_iota(jnp.int32, (half, lanes), 1) < width
+    pair_total, pb_count, piece, lanes = out_ref.shape
+    rows = pl.ds(pl.multiple_of(lax.axis_index("row") * piece, piece), piece)
+    low = lax.broadcasted_iota(jnp.int32, (piece, lanes), 1) < width
 
     def fetch(k, want):
         slot = slot_ref[k]
@@ -36,16 +35,21 @@
 
 
 def main_kernel(dims, picked, kern, out, w, basis, rows_r, rows_l, rows_t, f1, f2s, f2r, cbuf,
-                w_sem, d_send, d_recv, g_send, g_recv, s_send, s_recv, c_send, c_recv):
-    pb_count, row_devices, pair_total, half, tile, width = dims
+                w_sem, d_send, d_recv, g_send, g_recv, h_send, h_recv, y_send, y_recv,
+                s_send, s_recv, c_send, c_recv):
+    pb_count, row_devices, pair_total, piece, width = dims
     pb, row = lax.axis_index("pb"), lax.axis_index("row")
-    part = lax.rem(row, 2)
+    chips = row_devices // 2
+    part, chip = lax.rem(row, 2), lax.div(row, 2)
     mate = row + 1 - 2 * part
-    row_count, point_total = w.shape
+    row_count = w.shape[0]
     lanes = basis.shape[2]
     share = row_count // pb_count
-    tiles = point_total // tile
-    per_chunk = row_count // tile
+    order = [(e, flip) for e in range(1, chips) for flip in (0, 1)] + [(0, 1), (0, 0)]
+
+    def peer(e, flip):
+        side = 1 - part if flip else part
+        return 2 * lax.rem(chip + e, chips) + side
 
     w_copy = pltpu.make_async_copy(kern.at[0], w, w_sem)
     w_copy.start()
@@ -64,30 +68,44 @@
     lax.fori_loop(1, row_devices, greet_row, 0)
     pl.semaphore_wait(barrier, pb_count + row_devices - 2)
 
-    def block_rows(j, which):
-        return pl.ds(pl.multiple_of((j * 2 + which) * half, half), half)
+    def spot(p, j, which):
+        return basis.at[p, pl.ds(pl.multiple_of((j * row_devices + which) * piece, piece), piece)]
+
+    def source(d):
+        return lax.rem(pb + pb_count - d, pb_count)
 
     def own(p):
-        return pltpu.make_async_copy(picked.at[p, pb], basis.at[p, block_rows(pb, part)], d_recv.at[p, 0])
+        return pltpu.make_async_copy(picked.at[p, pb], spot(p, pb, row), d_recv.at[p, 0])
 
     def direct(p, d):
         q = lax.rem(pb + d, pb_count)
         return pltpu.make_async_remote_copy(
-            src_ref=picked.at[p, q], dst_ref=basis.at[p, block_rows(pb, part)],
+            src_ref=picked.at[p, q], dst_ref=spot(p, pb, row),
             send_sem=d_send.at[p, d], recv_sem=d_recv.at[p, d],
             device_id=(q, row), device_id_type=MESH)
 
-    def relay(p, d):
-        j = lax.rem(pb + pb_count - d, pb_count)
-        spot = basis.at[p, block_rows(j, part)]
-        return pltpu.make_async_remote_copy(
-            src_ref=spot, dst_ref=spot, send_sem=g_send.at[p, d], recv_sem=g_recv.at[p, d],
+    def across(p, e, d):
+        block = spot(p, source(d), row)
+        return pltpu.make_async_remote_copy(
+            src_ref=block, dst_ref=block, send_sem=y_send.at[p, e - 1, d], recv_sem=y_recv.at[p, e - 1, d],
+            device_id=(pb, peer(e, 0)), device_id_type=MESH)
+
+    def to_mate(p, d):
+        block = spot(p, source(d), row)
+        return pltpu.make_async_remote_copy(
+            src_ref=block, dst_ref=block, send_sem=g_send.at[p, d], recv_sem=g_recv.at[p, d],
             device_id=(pb, mate), device_id_type=MESH)
 
-    def shed(p, d):
-        to = lax.rem(row + d, row_devices)
-        return pltpu.make_async_remote_copy(
-            src_ref=f2s.at[p, to], dst_ref=f2r.at[p, d], send_sem=s_send.at[p, d], recv_sem=s_recv.at[p, d],
+    def onward(p, e, d):
+        block = spot(p, source(d), peer(chips - e, 0))
+        return pltpu.make_async_remote_copy(
+            src_ref=block, dst_ref=block, send_sem=h_send.at[p, e - 1, d], recv_sem=h_recv.at[p, e - 1, d],
+            device_id=(pb, mate), device_id_type=MESH)
+
+    def shed(p, s):
+        to = peer(*order[s])
+        return pltpu.make_async_remote_copy(
+            src_ref=f2s.at[p, s], dst_ref=f2r.at[p, s], send_sem=s_send.at[p, s], recv_sem=s_recv.at[p, s],
             device_id=(pb, to), device_id_type=MESH)
 
     def c_rows(j):
@@ -114,84 +132,103 @@
 
     loop(0, pair_total, send_pair)
 
-    def relay_pair(p):
+    def spread(p):
+        def pass_on(d):
+            for e in range(1, chips):
+                across(p, e, d).start()
+            to_mate(p, d).start()
+
         own(p).wait()
-        relay(p, 0).start()
+        pass_on(0)
 
         def one(d):
             direct(p, d).wait_recv()
-            relay(p, d).start()
+            pass_on(d)
 
         loop(1, pb_count, one)
 
+    def pass_far(p):
+        for e in range(1, chips):
+            def one(d):
+                across(p, e, d).wait_recv()
+                onward(p, e, d).start()
+
+            loop(0, pb_count, one)
+
     low = lax.broadcasted_iota(jnp.int32, (row_count, lanes), 1) < width
 
     def finish_pair(p):
-        total = f2s[p, row].astype(F32)
-        for d in range(1, row_devices):
-            shed(p, d).wait_recv()
-            total = total + f2r[p, d].astype(F32)
+        total = f2s[p, row_devices - 1].astype(F32)
+        for s in range(row_devices - 1):
+            shed(p, s).wait_recv()
+            total = total + f2r[p, s].astype(F32)
         stacked = jnp.concatenate([jnp.zeros_like(total), total], axis=0)
         cbuf[p] = jnp.where(low, f1[p], stacked.T).astype(BF16)
+        loop(1, pb_count, lambda d: give(p, d).start())
         own_c(p).start()
-        loop(1, pb_count, lambda d: give(p, d).start())
-
-    def tiles_of(p, start, stop):
-        def one(t):
-            cols = pl.ds(pl.multiple_of(t * tile, tile), tile)
-            there = basis[p, cols, :]
-            second = None
-            chunk = row_count // 2
-            for m in range(2):
-                here = slice(m * chunk, (m + 1) * chunk)
-                weight = w[here, cols].astype(F32)
-                gram = lax.dot_general(rows_r[here], there, NT, preferred_element_type=F32)
-                f1[p, here] += jnp.dot((weight * gram).astype(BF16), there, preferred_element_type=F32)
-                gram = lax.dot_general(rows_l[here], there, NT, preferred_element_type=F32)
-                term = jnp.dot(rows_t[:, here], (weight * gram).astype(BF16), preferred_element_type=F32)
-                second = term if second is None else second + term
-            inner = pl.ds(pl.multiple_of(lax.rem(t, per_chunk) * tile, tile), tile)
-            f2s[p, lax.div(t, per_chunk), :, inner] = second[width:].astype(BF16)
-
-        loop(start, stop, one)
-
-    relay_pair(0)
+
+    def tile_of(p, s):
+        cols = pl.ds(pl.multiple_of(peer(*order[s]) * row_count, row_count), row_count)
+        there = basis[p, cols, :]
+        second = None
+        chunk = row_count // 2
+        for m in range(2):
+            here = slice(m * chunk, (m + 1) * chunk)
+            weight = w[here, cols].astype(F32)
+            gram = lax.dot_general(rows_r[here], there, NT, preferred_element_type=F32)
+            first = jnp.dot((weight * gram).astype(BF16), there, preferred_element_type=F32)
+            f1[p, here] = first if s == 0 else f1[p, here] + first
+            gram = lax.dot_general(rows_l[here], there, NT, preferred_element_type=F32)
+            term = jnp.dot(rows_t[:, here], (weight * gram).astype(BF16), preferred_element_type=F32)
+            second = term if second is None else second + term
+        f2s[p, s] = second[width:].astype(BF16)
+        if s < row_devices - 1:
+            shed(p, s).start()
+
+    spread(0)
+    pass_far(0)
     w_copy.wait()
 
     def pair_step(p):
-        loop(0, pb_count, lambda d: relay(p, d).wait_recv())
-        mine = basis[p, pl.ds(pl.multiple_of(row * row_count, row_count), row_count), :]
-        rows_r[...] = jnp.where(low, 0, mine.astype(F32)).astype(BF16)
-        rows_l[...] = jnp.where(low, mine.astype(F32), 0).astype(BF16)
-        rows_t[...] = mine.astype(F32).T.astype(BF16)
-        f1[p] = jnp.zeros((row_count, lanes), F32)
-        tiles_of(p, 0, tiles // 2)
-
-        @pl.when(p + 1 < pair_total)
-        def _():
-            relay_pair(p + 1)
-
-        @pl.when(p > 0)
-        def _():
-            finish_pair(p - 1)
-
-        tiles_of(p, tiles // 2, tiles)
-        loop(1, row_devices, lambda d: shed(p, d).start())
+        def arrive(d):
+            to_mate(p, d).wait_recv()
+            for e in range(1, chips):
+                onward(p, e, d).wait_recv()
+
+        loop(0, pb_count, arrive)
+        mine = basis[p, pl.ds(pl.multiple_of(row * row_count, row_count), row_count), :].astype(F32)
+        rows_r[...] = jnp.where(low, 0, mine).astype(BF16)
+        rows_l[...] = jnp.where(low, mine, 0).astype(BF16)
+        rows_t[...] = mine.T.astype(BF16)
+        for s in range(row_devices):
+            tile_of(p, s)
+            if s == 0:
+                pl.when(p + 1 < pair_total)(lambda: spread(p + 1))
+                pl.when(p > 0)(lambda: finish_pair(p - 1))
+            if s == row_devices - 2:
+                pl.when(p + 1 < pair_total)(lambda: pass_far(p + 1))
 
     loop(0, pair_total, pair_step)
     finish_pair(pair_total - 1)
 
     def settle(p):
         own_c(p).wait()
-        relay(p, 0).wait_send()
+
+        def relayed(d):
+            to_mate(p, d).wait_send()
+            for e in range(1, chips):
+                across(p, e, d).wait_send()
+                onward(p, e, d).wait_send()
+
+        loop(0, pb_count, relayed)
 
         def one(d):
             direct(p, d).wait_send()
-            relay(p, d).wait_send()
             give(p, d).wait()
 
         loop(1, pb_count, one)
-        loop(1, row_devices, lambda d: shed(p, d).wait_send())
+        for s in range(row_devices - 1):
+            shed(p, s).wait_send()
 
     loop(0, pair_total, settle)
 
@@ -228,21 +265,21 @@
     k_total = k_slot.shape[0]
     width = orbitals.shape[1] // k_total
     lanes = 2 * width
-    half = orbitals.shape[0] // 2
+    piece = orbitals.shape[0] // row_devices
+    far = max(row_devices // 2 - 1, 1)
     share = row_count // pb_count
-    tile = row_count // 2
     smem = pl.BlockSpec(memory_space=pltpu.SMEM)
     vmem = pl.BlockSpec(memory_space=pltpu.VMEM)
     hbm = pl.BlockSpec(memory_space=pl.ANY)
     picked = pl.pallas_call(
         functools.partial(pick_kernel, width),
-        out_shape=jax.ShapeDtypeStruct((pair_total, pb_count, half, lanes), BF16),
+        out_shape=jax.ShapeDtypeStruct((pair_total, pb_count, piece, lanes), BF16),
         in_specs=[smem, smem, vmem],
         out_specs=vmem,
     )(pairs, k_slot, orbitals)
     sems = pltpu.SemaphoreType.DMA
     got = pl.pallas_call(
-        functools.partial(main_kernel, (pb_count, row_devices, pair_total, half, tile, width)),
+        functools.partial(main_kernel, (pb_count, row_devices, pair_total, piece, width)),
         out_shape=jax.ShapeDtypeStruct((pair_total, pb_count, share, lanes), BF16),
         in_specs=[hbm, hbm],
         out_specs=hbm,
@@ -261,6 +298,10 @@
             sems((pair_total, pb_count)),
             sems((pair_total, pb_count)),
             sems((pair_total, pb_count)),
+            sems((pair_total, far, pb_count)),
+            sems((pair_total, far, pb_count)),
+            sems((pair_total, far, pb_count)),
+            sems((pair_total, far, pb_count)),
             sems((pair_total, row_devices)),
             sems((pair_total, row_devices)),
             sems((pair_total, pb_count)),

time: 107 us -> 95.3 us (0.89)
  Pallas kernels: 105 us -> 93.8 us
    pallas_call x1, Pallas kernels: 94.1 us -> 83.7 us  [shards(): pl.pallas_call(functools.partial(main_kernel, (pb_count, row_devices, pai...]
where the time goes in v2:
time: 95.3 us; the launch traced here: 95.2 us
  Pallas kernels  93.8 us (98%)
  local copies, waits for them, and re-layouts  1.37 us (1%)
    pallas_call x1, Pallas kernels, shards(): pl.pallas_call(functools.partial(main_kernel, (pb_count, row_devices, pai...  83.7 us
    pallas_call x1, Pallas kernels, shards(): pl.pallas_call(functools.partial(pick_kernel, width), out_shape=jax.Shape...  5.51 us
    pallas_call x1, Pallas kernels, shards(): pl.pallas_call(functools.partial(combine_kernel, width), out_shape=jax.Sh...  4.53 us

profile of v2, /device:TPU:0, one launch (start us, length us, event | category | flops | bytes accessed | tf_op | source)
XLA Modules:
  0.0 95.2 jit_solution(17128147588479749490)
XLA Ops:
  0.0 1.4 %copy.7.pairs_ref = s32[8,4,2]{2,1,0:T(4,128)} copy(s32[8,4,2]{0,2,1:T(2,128)} %param.7) | data formatting | bytes 512 | tf_op args[2]
  1.4 5.5 %shard_map.55.picked = bf16[4,8,128,128]{3,2,1,0:T(8,128)(2,1)} custom-call(s32[8,4,2]{2,1,0:T(4,128)} %copy.7.pairs_ref, s32[16]{0:T(128)} %slot_ref.1, bf16[512,1024]{1,0:T(8,128)(2,1)} %orb_ref.1), custom_call_target="tpu_custom_call" | custom-call | tf_op jit(solution)/shard_map/pallas_call | solution.py:274
  6.9 83.7 %shard_map.56.got_ref = bf16[4,8,128,128]{3,2,1,0:T(8,128)(2,1)} custom-call(bf16[4,8,128,128]{3,2,1,0:T(8,128)(2,1)} %shard_map.55.picked, bf16[1,1024,4096]{2,1,0:T(8,128)(2,1)} %kern.1), custom_call_target="tpu_custom_call" | custom-call | tf_op jit(solution)/shard_map/pallas_call | solution.py:281
  90.6 4.5 %shard_map.57 = f32[1,128,1024]{2,1,0:T(8,128)} custom-call(s32[8,4,2]{2,1,0:T(4,128)} %copy.7.pairs_ref, s32[8]{0:T(128)} %count_ref.1, bf16[4,8,128,128]{3,2,1,0:T(8,128)(2,1)} %shard_map.56.got_ref), custom_call_target="tpu_custom_call" | custom-call | tf_op jit(solution)/shard_map/pallas_call | solution.py:314

commit v3 on v2

--- a/solution.py
+++ b/solution.py
@@ -24,14 +24,14 @@
         moved = pltpu.roll(block, width, 1)
         return jnp.where((slot & 1) == want, block, moved)
 
-    def step(n, carry):
-        q, p = lax.rem(n, pb_count), lax.div(n, pb_count)
-        left = fetch(pairs_ref[q, p, 0], 0)
-        right = fetch(pairs_ref[q, p, 1], 1)
-        out_ref[p, q] = jnp.where(low, left, right).astype(BF16)
+    def step(q, carry):
+        for p in range(pair_total):
+            left = fetch(pairs_ref[q, p, 0], 0)
+            right = fetch(pairs_ref[q, p, 1], 1)
+            out_ref[p, q] = jnp.where(low, left, right).astype(BF16)
         return carry
 
-    lax.fori_loop(0, pair_total * pb_count, step, 0)
+    lax.fori_loop(0, pb_count, step, 0)
 
 
 def main_kernel(dims, picked, kern, out, w, basis, rows_r, rows_l, rows_t, f1, f2s, f2r, cbuf,
@@ -43,7 +43,7 @@
     part, chip = lax.rem(row, 2), lax.div(row, 2)
     mate = row + 1 - 2 * part
     row_count = w.shape[0]
-    lanes = basis.shape[2]
+    lanes = basis.shape[4]
     share = row_count // pb_count
     order = [(e, flip) for e in range(1, chips) for flip in (0, 1)] + [(0, 1), (0, 0)]
 
@@ -69,10 +69,11 @@
     pl.semaphore_wait(barrier, pb_count + row_devices - 2)
 
     def spot(p, j, which):
-        return basis.at[p, pl.ds(pl.multiple_of((j * row_devices + which) * piece, piece), piece)]
-
-    def source(d):
-        return lax.rem(pb + pb_count - d, pb_count)
+        return basis.at[p, j, which]
+
+    def points(p, r):
+        span = pb_count // row_devices
+        return basis[p, pl.ds(r * span, span)].reshape(row_count, lanes)
 
     def own(p):
         return pltpu.make_async_copy(picked.at[p, pb], spot(p, pb, row), d_recv.at[p, 0])
@@ -84,22 +85,22 @@
             send_sem=d_send.at[p, d], recv_sem=d_recv.at[p, d],
             device_id=(q, row), device_id_type=MESH)
 
-    def across(p, e, d):
-        block = spot(p, source(d), row)
-        return pltpu.make_async_remote_copy(
-            src_ref=block, dst_ref=block, send_sem=y_send.at[p, e - 1, d], recv_sem=y_recv.at[p, e - 1, d],
+    def across(p, e):
+        block = basis.at[p, :, row]
+        return pltpu.make_async_remote_copy(
+            src_ref=block, dst_ref=block, send_sem=y_send.at[p, e - 1], recv_sem=y_recv.at[p, e - 1],
             device_id=(pb, peer(e, 0)), device_id_type=MESH)
 
-    def to_mate(p, d):
-        block = spot(p, source(d), row)
-        return pltpu.make_async_remote_copy(
-            src_ref=block, dst_ref=block, send_sem=g_send.at[p, d], recv_sem=g_recv.at[p, d],
+    def to_mate(p):
+        block = basis.at[p, :, row]
+        return pltpu.make_async_remote_copy(
+            src_ref=block, dst_ref=block, send_sem=g_send.at[p], recv_sem=g_recv.at[p],
             device_id=(pb, mate), device_id_type=MESH)
 
-    def onward(p, e, d):
-        block = spot(p, source(d), peer(chips - e, 0))
-        return pltpu.make_async_remote_copy(
-            src_ref=block, dst_ref=block, send_sem=h_send.at[p, e - 1, d], recv_sem=h_recv.at[p, e - 1, d],
+    def onward(p, e):
+        block = basis.at[p, :, peer(chips - e, 0)]
+        return pltpu.make_async_remote_copy(
+            src_ref=block, dst_ref=block, send_sem=h_send.at[p, e - 1], recv_sem=h_recv.at[p, e - 1],
             device_id=(pb, mate), device_id_type=MESH)
 
     def shed(p, s):
@@ -133,27 +134,16 @@
     loop(0, pair_total, send_pair)
 
     def spread(p):
-        def pass_on(d):
-            for e in range(1, chips):
-                across(p, e, d).start()
-            to_mate(p, d).start()
-
         own(p).wait()
-        pass_on(0)
-
-        def one(d):
-            direct(p, d).wait_recv()
-            pass_on(d)
-
-        loop(1, pb_count, one)
+        loop(1, pb_count, lambda d: direct(p, d).wait_recv())
+        for e in range(1, chips):
+            across(p, e).start()
+        to_mate(p).start()
 
     def pass_far(p):
         for e in range(1, chips):
-            def one(d):
-                across(p, e, d).wait_recv()
-                onward(p, e, d).start()
-
-            loop(0, pb_count, one)
+            across(p, e).wait_recv()
+            onward(p, e).start()
 
     low = lax.broadcasted_iota(jnp.int32, (row_count, lanes), 1) < width
 
@@ -168,8 +158,9 @@
         own_c(p).start()
 
     def tile_of(p, s):
-        cols = pl.ds(pl.multiple_of(peer(*order[s]) * row_count, row_count), row_count)
-        there = basis[p, cols, :]
+        to = peer(*order[s])
+        cols = pl.ds(pl.multiple_of(to * row_count, row_count), row_count)
+        there = points(p, to)
         second = None
         chunk = row_count // 2
         for m in range(2):
@@ -190,13 +181,10 @@
     w_copy.wait()
 
     def pair_step(p):
-        def arrive(d):
-            to_mate(p, d).wait_recv()
-            for e in range(1, chips):
-                onward(p, e, d).wait_recv()
-
-        loop(0, pb_count, arrive)
-        mine = basis[p, pl.ds(pl.multiple_of(row * row_count, row_count), row_count), :].astype(F32)
+        to_mate(p).wait_recv()
+        for e in range(1, chips):
+            onward(p, e).wait_recv()
+        mine = points(p, row).astype(F32)
         rows_r[...] = jnp.where(low, 0, mine).astype(BF16)
         rows_l[...] = jnp.where(low, mine, 0).astype(BF16)
         rows_t[...] = mine.T.astype(BF16)
@@ -214,13 +202,10 @@
     def settle(p):
         own_c(p).wait()
 
-        def relayed(d):
-            to_mate(p, d).wait_send()
-            for e in range(1, chips):
-                across(p, e, d).wait_send()
-                onward(p, e, d).wait_send()
-
-        loop(0, pb_count, relayed)
+        to_mate(p).wait_send()
+        for e in range(1, chips):
+            across(p, e).wait_send()
+            onward(p, e).wait_send()
 
         def one(d):
             direct(p, d).wait_send()
@@ -285,7 +270,7 @@
         out_specs=hbm,
         scratch_shapes=[
             pltpu.VMEM((row_count, point_total), BF16),
-            pltpu.VMEM((pair_total, point_total, lanes), BF16),
+            pltpu.VMEM((pair_total, pb_count, row_devices, piece, lanes), BF16),
             pltpu.VMEM((row_count, lanes), BF16),
             pltpu.VMEM((row_count, lanes), BF16),
             pltpu.VMEM((lanes, row_count), BF16),
@@ -296,12 +281,12 @@
             sems,
             sems((pair_total, pb_count)),
             sems((pair_total, pb_count)),
-            sems((pair_total, pb_count)),
-            sems((pair_total, pb_count)),
-            sems((pair_total, far, pb_count)),
-            sems((pair_total, far, pb_count)),
-            sems((pair_total, far, pb_count)),
-            sems((pair_total, far, pb_count)),
+            sems((pair_total,)),
+            sems((pair_total,)),
+            sems((pair_total, far)),
+            sems((pair_total, far)),
+            sems((pair_total, far)),
+            sems((pair_total, far)),
             sems((pair_total, row_devices)),
             sems((pair_total, row_devices)),
             sems((pair_total, pb_count)),

time: 95.3 us -> 93.9 us (0.985)
  Pallas kernels: 93.8 us -> 91.9 us
    pallas_call x1, Pallas kernels: 5.51 us -> 3.48 us  [shards(): pl.pallas_call(functools.partial(pick_kernel, width), out_shape=jax.Shape...]
where the time goes in v3:
time: 93.9 us; the launch traced here: 93.3 us
  Pallas kernels  91.9 us (98%)
  local copies, waits for them, and re-layouts  1.37 us (1%)
    pallas_call x1, Pallas kernels, shards(): pl.pallas_call(functools.partial(main_kernel, (pb_count, row_devices, pai...  84.4 us
    pallas_call x1, Pallas kernels, shards(): pl.pallas_call(functools.partial(combine_kernel, width), out_shape=jax.Sh...  4.09 us
    pallas_call x1, Pallas kernels, shards(): pl.pallas_call(functools.partial(pick_kernel, width), out_shape=jax.Shape...  3.48 us

profile of v3, /device:TPU:0, one launch (start us, length us, event | category | flops | bytes accessed | tf_op | source)
XLA Modules:
  0.0 93.3 jit_solution(2685462597049783628)
XLA Ops:
  0.0 1.4 %copy.7.pairs_ref = s32[8,4,2]{2,1,0:T(4,128)} copy(s32[8,4,2]{0,2,1:T(2,128)} %param.7) | data formatting | bytes 512 | tf_op args[2]
  1.4 3.5 %shard_map.55.picked = bf16[4,8,128,128]{3,2,1,0:T(8,128)(2,1)} custom-call(s32[8,4,2]{2,1,0:T(4,128)} %copy.7.pairs_ref, s32[16]{0:T(128)} %slot_ref.1, bf16[512,1024]{1,0:T(8,128)(2,1)} %orb_ref.1), custom_call_target="tpu_custom_call" | custom-call | tf_op jit(solution)/shard_map/pallas_call | solution.py:259
  4.9 84.4 %shard_map.56.got_ref = bf16[4,8,128,128]{3,2,1,0:T(8,128)(2,1)} custom-call(bf16[4,8,128,128]{3,2,1,0:T(8,128)(2,1)} %shard_map.55.picked, bf16[1,1024,4096]{2,1,0:T(8,128)(2,1)} %kern.1), custom_call_target="tpu_custom_call" | custom-call | tf_op jit(solution)/shard_map/pallas_call | solution.py:266
  89.2 4.1 %shard_map.57 = f32[1,128,1024]{2,1,0:T(8,128)} custom-call(s32[8,4,2]{2,1,0:T(4,128)} %copy.7.pairs_ref, s32[8]{0:T(128)} %count_ref.1, bf16[4,8,128,128]{3,2,1,0:T(8,128)(2,1)} %shard_map.56.got_ref), custom_call_target="tpu_custom_call" | custom-call | tf_op jit(solution)/shard_map/pallas_call | solution.py:299

commit v4 on v3

--- a/solution.py
+++ b/solution.py
@@ -223,12 +223,10 @@
     low = lax.broadcasted_iota(jnp.int32, (share, lanes), 1) < width
     out_ref[...] = jnp.zeros_like(out_ref)
 
-    def step(n, carry):
-        q, p = lax.rem(n, pb_count), lax.div(n, pb_count)
-
-        @pl.when(p < count_ref[q])
-        def _():
-            block = got_ref[p, q].astype(F32)
+    def step(q, carry):
+        for p in range(pair_total):
+            live = p < count_ref[q]
+            block = jnp.where(live, got_ref[p, q].astype(F32), 0.0)
             moved = pltpu.roll(block, width, 1)
             for side in range(2):
                 k = pairs_ref[q, p, side]
@@ -237,10 +235,9 @@
                 value = jnp.where(low == (odd == 0), value, 0.0)
                 spot = pl.ds(pl.multiple_of((k >> 1) * lanes, lanes), lanes)
                 out_ref[0, :, spot] += value
-
         return carry
 
-    lax.fori_loop(0, pair_total * pb_count, step, 0)
+    lax.fori_loop(0, pb_count, step, 0)
 
 
 def shards(kernels, orbitals, pairs, k_slot, pair_count):

time: 93.9 us -> 93.1 us (level)
  no operation moved by 1% of the time
where the time goes in v4:
time: 93.1 us; the launch traced here: 92.8 us
  Pallas kernels  91.4 us (98%)
  local copies, waits for them, and re-layouts  1.37 us (1%)
    pallas_call x1, Pallas kernels, shards(): pl.pallas_call(functools.partial(main_kernel, (pb_count, row_devices, pai...  84.4 us
    pallas_call x1, Pallas kernels, shards(): pl.pallas_call(functools.partial(combine_kernel, width), out_shape=jax.Sh...  3.55 us
    pallas_call x1, Pallas kernels, shards(): pl.pallas_call(functools.partial(pick_kernel, width), out_shape=jax.Shape...  3.48 us

profile of v4, /device:TPU:0, one launch (start us, length us, event | category | flops | bytes accessed | tf_op | source)
XLA Modules:
  0.0 92.8 jit_solution(5193693537565913592)
XLA Ops:
  0.0 1.4 %copy.7.pairs_ref = s32[8,4,2]{2,1,0:T(4,128)} copy(s32[8,4,2]{0,2,1:T(2,128)} %param.7) | data formatting | bytes 512 | tf_op args[2]
  1.4 3.5 %shard_map.55.picked = bf16[4,8,128,128]{3,2,1,0:T(8,128)(2,1)} custom-call(s32[8,4,2]{2,1,0:T(4,128)} %copy.7.pairs_ref, s32[16]{0:T(128)} %slot_ref.1, bf16[512,1024]{1,0:T(8,128)(2,1)} %orb_ref.1), custom_call_target="tpu_custom_call" | custom-call | tf_op jit(solution)/shard_map/pallas_call | solution.py:256
  4.9 84.4 %shard_map.56.got_ref = bf16[4,8,128,128]{3,2,1,0:T(8,128)(2,1)} custom-call(bf16[4,8,128,128]{3,2,1,0:T(8,128)(2,1)} %shard_map.55.picked, bf16[1,1024,4096]{2,1,0:T(8,128)(2,1)} %kern.1), custom_call_target="tpu_custom_call" | custom-call | tf_op jit(solution)/shard_map/pallas_call | solution.py:263
  89.2 3.6 %shard_map.57 = f32[1,128,1024]{2,1,0:T(8,128)} custom-call(s32[8,4,2]{2,1,0:T(4,128)} %copy.7.pairs_ref, s32[8]{0:T(128)} %count_ref.1, bf16[4,8,128,128]{3,2,1,0:T(8,128)(2,1)} %shard_map.56.got_ref), custom_call_target="tpu_custom_call" | custom-call | tf_op jit(solution)/shard_map/pallas_call | solution.py:296
